TPU v7x, 32 devices: a whole 2x2x4 slice. The times are simulated.
32 devices in a mesh: wide: 4 (over z), narrow: 8 (over y, x, core).
Axes of the slice: x: 2, y: 2, z: 4, core: 2. Of those that a mesh axis runs over, the one named last changes fastest.
Arguments:
- src_design: float32 [5, 4194304], P(None, ('wide', 'narrow')), may hold values from -6 to 6
- att_design: float32 [16, 4194304], P(None, ('wide', 'narrow')), may hold values from -3 to 3
- right_side: float32 [4194304], P(('wide', 'narrow')), may hold values from -6 to 6
- block_source: int32 [65536], P(('wide', 'narrow')), may hold values from 0 to 65535, as said below
- block_segment: int32 [65536], P(('wide', 'narrow')), may hold values from 0 to 8191, as said below
- block_count: int32 [65536], P(('wide', 'narrow')), may hold values from 8 to 64
Outputs:
- sol_src: float32 [5, 65536], P(None, ('wide', 'narrow'))
- sol_att: float32 [16, 8192], P(None, 'narrow')
- dir_src: float32 [5, 65536], P(None, ('wide', 'narrow'))
- dir_att: float32 [16, 8192], P(None, 'narrow')
Inputs may be any that keep to these rules, and one draw needn't show every extreme that they name: `block_source`: A block held by the device at index w of wide names a source in [w * 2048 * 8, (w + 1) * 2048 * 8); of the 2048 blocks of one device, exactly 2048 / 8 name sources in [(w * 8 + m) * 2048, (w * 8 + m + 1) * 2048) for each m in 0 to 8 - 1; the lowest and highest source of the partition are named on every device. `block_segment`: A block held by the device at index n of narrow names a segment in [n * 1024, (n + 1) * 1024); the lowest and highest of that range are named on every device.
All inputs are finite; a program needn't handle non-finite values.
Results may differ from a plain program's by a relative error of at most 0.00018.
Values sent between devices are 32-bit elements; how exact they have to be, the bound alone decides.
No kernel may reach another device: no remote copies, remote signals or barrier semaphores. Data moves between devices by JAX's collectives and lax.ppermute only.
A program may use at most 192 MiB of HBM per device.

v0:
```python
import functools

import jax
import jax.numpy as jnp
from jax import lax
from jax.experimental import pallas as pl
from jax.experimental.pallas import tpu as pltpu
from jax.sharding import PartitionSpec as P


SRC_DEV = 2048
SEG_DEV = 1024
LANE = 128
HIGH = 256
F32 = jnp.float32
BF16 = jnp.bfloat16
I32 = jnp.int32
MIB = 1 << 20
PERIOD = 7


def lanes_of(values, index):
    return jnp.take_along_axis(values, index, axis=1, mode="promise_in_bounds")


def row_iota(rows, columns=LANE):
    return lax.broadcasted_iota(I32, (rows, columns), 0)


def lane_iota(rows, columns=LANE):
    return lax.broadcasted_iota(I32, (rows, columns), 1)


def to_tiles(rows):
    count = rows.shape[0]
    lane = lane_iota(count)
    first = lanes_of(rows, (2 * lane) % LANE)
    second = lanes_of(rows, (2 * lane + 1) % LANE)
    head = lane < LANE // 2
    even = jnp.where(head, first, pltpu.roll(first, count - 1, 0))
    odd = jnp.where(head, pltpu.roll(second, 1, 0), second)
    return jnp.where(row_iota(count) % 2 == 0, even, odd)


def split_three(values):
    top = values.astype(BF16).astype(F32)
    rest = values - top
    middle = rest.astype(BF16).astype(F32)
    return top, middle, rest - middle


def spread_rows(store, picked, row, column, levels):
    rows = picked.shape[0]
    size = levels * rows
    levels_at = (row_iota(size) // rows).astype(F32).astype(BF16)
    named = jnp.broadcast_to(row.astype(F32), (size, LANE)).astype(BF16)
    mask = jnp.where(levels_at == named, jnp.ones((), BF16), jnp.zeros((), BF16))
    for part, piece in enumerate(split_three(picked)):
        whole = jnp.concatenate([piece] * (16 // rows), axis=0).astype(BF16)
        whole = jnp.concatenate([whole] * (size // 16), axis=0)
        store[pl.ds(part * size, size), pl.ds(column, LANE)] = whole * mask


def fold_rows(values):
    total = values[0:8]
    for at in range(8, values.shape[0], 8):
        total = total + values[at : at + 8]
    return total


def row_sums(sums):
    rows = sums.shape[0] // 8
    total = sums[pl.ds(0, rows, stride=8), :]
    for at in range(1, 8):
        total = total + sums[pl.ds(at, rows, stride=8), :]
    return total


def rank_blocks(narrow, source_ref, segment_ref, pos_ref, seg_ref, order_ref, ids_ref, left, right):
    tiles = source_ref.shape[0]
    cap = tiles * LANE // narrow
    local = to_tiles(source_ref[...]) & (SRC_DEV * narrow - 1)
    seg_ref[...] = to_tiles(segment_ref[...]) & (SEG_DEV - 1)
    owner = local // SRC_DEV
    inner = local & (SRC_DEV - 1)
    marks = jnp.concatenate([jnp.where(owner == m, 1.0, 0.0) for m in range(narrow)], axis=0)
    marks = marks.astype(BF16)
    total = narrow * tiles
    before = jnp.where(row_iota(LANE) < lane_iota(LANE), 1.0, 0.0).astype(BF16)
    in_row = jnp.dot(marks, before, preferred_element_type=F32)
    at_row, at_lane = row_iota(total, total), lane_iota(total, total)
    earlier = (at_row // tiles == at_lane // tiles) & (at_lane < at_row)
    ahead = jnp.dot(jnp.where(earlier, 1.0, 0.0).astype(BF16), marks, preferred_element_type=F32)
    ahead = jnp.dot(ahead.astype(BF16), jnp.ones((LANE, LANE), BF16), preferred_element_type=F32)
    rank = (in_row + ahead).astype(I32)
    pos = jnp.zeros((tiles, LANE), I32)
    for m in range(narrow):
        pos = jnp.where(owner == m, m * cap + rank[m * tiles : (m + 1) * tiles], pos)
    pos_ref[...] = pos
    levels = tiles * LANE // HIGH
    lane = lane_iota(1).astype(F32)
    for t in range(tiles):
        here = pos[t : t + 1]
        level = row_iota(levels) == here // HIGH
        mine = inner[t : t + 1]
        pieces = (
            jnp.full((1, LANE), float(t), F32),
            lane,
            (mine // LANE).astype(F32),
            (mine % LANE).astype(F32),
        )
        for part, piece in enumerate(pieces):
            left[part * levels : (part + 1) * levels, t * LANE : (t + 1) * LANE] = jnp.where(
                level, piece, 0.0
            ).astype(BF16)
    mark_high(right, pos)
    found = jnp.dot(left[0 : 4 * levels, :], right[...], preferred_element_type=F32)
    tile_at, lane_at = found[:levels], found[levels : 2 * levels]
    order = (tile_at * LANE + lane_at).astype(I32)
    ids = found[2 * levels : 3 * levels] * LANE + found[3 * levels :]
    for level in range(levels):
        for half in range(HIGH // LANE):
            row = level * (HIGH // LANE) + half
            cut = slice(half * LANE, (half + 1) * LANE)
            order_ref[row : row + 1, :] = order[level : level + 1, cut]
            ids_ref[row : row + 1, :] = ids[level : level + 1, cut]


def mark_high(right, index):
    columns = (index & (HIGH - 1)).astype(F32).T
    high_at = lane_iota(LANE, HIGH).astype(F32).astype(BF16)
    one, zero = jnp.ones((), BF16), jnp.zeros((), BF16)
    for t in range(index.shape[0]):
        here = jnp.broadcast_to(columns[:, t : t + 1], (LANE, HIGH)).astype(BF16)
        right[t * LANE : (t + 1) * LANE, :] = jnp.where(high_at == here, one, zero)


def fill_att(blocks, seg_ref, left, t):
    here = seg_ref[pl.ds(t, 1), :]
    column = pl.multiple_of(t * LANE, LANE)
    spread_rows(left, blocks[t, 0:16, :], here // HIGH, column, SEG_DEV // HIGH)


def scatter_att(out_ref, left, right):
    levels = SEG_DEV // HIGH
    sums = jnp.dot(left[...], right[...], preferred_element_type=F32)
    size = 16 * levels
    sums = sums[:size] + (sums[size : 2 * size] + sums[2 * size :])
    for level in range(levels):
        out_ref[:, level * HIGH : (level + 1) * HIGH] = sums[level * 16 : (level + 1) * 16]


def pick(tables, count, index):
    low = index & (LANE - 1)
    high = index // LANE
    rows = tables(0).shape[0]
    low = jnp.broadcast_to(low, (rows, LANE))
    out = lanes_of(tables(0), low)
    for c in range(1, count):
        out = jnp.where(high == c, lanes_of(tables(c), low), out)
    return out


def send_sorted(narrow, blocks, order_ref, extra, out_ref):
    tiles = order_ref.shape[0]
    cap = tiles * LANE // narrow
    per = cap // LANE
    keep = row_iota(8) < 5
    for t in range(tiles):
        values = pick(lambda c: blocks[c, 16:24, :], tiles, order_ref[t : t + 1, :])
        values = jnp.where(keep, values, extra(t))
        out_ref[t // per, :, (t % per) * LANE : (t % per + 1) * LANE] = values


def entry(ref, per, t):
    return ref[t // per, :, (t % per) * LANE : (t % per + 1) * LANE]


def start_kernel(
    narrow,
    att_hbm, src_hbm, rhs_hbm, source_hbm, segment_hbm, count_hbm,
    table_ref, square_ref, pos_ref, seg_ref, order_ref, right, att_ref, send_ref,
    att_in, src_in, rhs_in, source_in, segment_in, count_in, blocks, ids, sums, same, left, sems, int_sems,
):
    groups, att_sets = att_in.shape[0], att_in.shape[1]
    att_rows, src_rows = att_sets * 8, src_hbm.shape[1]
    att_flat = att_in.reshape(groups * att_sets * LANE * 8, LANE)
    src_flat = src_in.reshape(groups * LANE * 8, LANE)
    obs = table_ref.shape[2]

    def ints():
        pairs = ((source_hbm, source_in), (segment_hbm, segment_in), (count_hbm, count_in))
        return [
            pltpu.make_async_copy(one, two, int_sems.at[at]) for at, (one, two) in enumerate(pairs)
        ]

    def loads(g):
        cut = pl.ds(g * LANE, LANE)
        return [
            pltpu.make_async_copy(att_hbm.at[:, cut], att_in.at[g], sems.at[0, g]),
            pltpu.make_async_copy(src_hbm.at[cut], src_in.at[g, :, 0:src_rows], sems.at[1, g]),
            pltpu.make_async_copy(rhs_hbm.at[cut], rhs_in.at[g], sems.at[2, g]),
        ]

    def begin(g, carry):
        for one in loads(g):
            one.start()
        return carry

    for one in ints():
        one.start()
    lax.fori_loop(0, groups, begin, 0)
    for one in ints():
        one.wait()
    count_in[...] = to_tiles(count_in[...])
    square_ref[...] = jnp.zeros_like(square_ref)
    sums[...] = jnp.zeros_like(sums)
    diagonal = jnp.where(row_iota(LANE) == lane_iota(LANE), 1.0, 0.0).astype(BF16)
    for part in range(3):
        same[:, part * LANE : (part + 1) * LANE] = diagonal
    rank_blocks(narrow, source_in, segment_in, pos_ref, seg_ref, order_ref, ids, left, right)
    mark_high(right, seg_ref[...])
    place = row_iota(obs)

    def turn(g, carry):
        for half in range(2):
            fill_att(blocks, seg_ref, left, jnp.maximum(g * 2 - 2 + half, half))
        for one in loads(g):
            one.wait()
        wide_rhs = rhs_in[g].T
        live, rhs = [], []
        for half in range(2):
            alive = place < count_in[pl.ds(g * 2 + half, 1), :]
            live.append(alive)
            part = jnp.where(alive, wide_rhs[half * obs : half * obs + obs], 0.0)
            rhs.append(part)
            square_ref[...] += fold_rows(part * part)

        def rows_of(i):
            if i < att_rows:
                base = pl.multiple_of((g * att_sets + i // 8) * (LANE * 8), LANE * 8)
                return att_flat[pl.ds(base + i % 8, LANE, stride=8), :]
            base = pl.multiple_of(g * (LANE * 8), LANE * 8)
            return src_flat[pl.ds(base + i - att_rows, LANE, stride=8), :]

        def keep(i, turned):
            for half in range(2):
                part = jnp.where(live[half], turned[half * obs : half * obs + obs], 0.0)
                table_ref[g * 2 + half, i] = part
                sums[half, i * 8 : i * 8 + 8, :] = fold_rows(part * rhs[half])

        total = att_rows + src_rows
        i = 0
        while i < total:
            if i % PERIOD == 0 and i + 1 < total:
                both = jnp.concatenate([rows_of(i), rows_of(i + 1)], axis=0)
                split = jnp.concatenate([part.astype(BF16) for part in split_three(both)], axis=1)
                turned = lax.dot_general(
                    same[...], split, (((1,), (1,)), ((), ())), preferred_element_type=F32
                )
                keep(i, turned[:, :LANE])
                keep(i + 1, turned[:, LANE:])
                i += 2
            else:
                keep(i, rows_of(i).T)
                i += 1
        for half in range(2):
            blocks[g * 2 + half] = row_sums(sums.at[half])
        return carry

    lax.fori_loop(0, groups, turn, 0)
    for half in range(2):
        fill_att(blocks, seg_ref, left, groups * 2 - 2 + half)
    scatter_att(att_ref, left, right)
    lane = lane_iota(16)
    att_ref[:, SEG_DEV:] = jnp.where(lane == 0, jnp.sum(square_ref[...]), 0.0)
    row = row_iota(8)
    send_sorted(
        narrow,
        blocks,
        order_ref,
        lambda t: jnp.where(row == 5, ids[t : t + 1, :], 0.0),
        send_ref,
    )


def owner_kernel(narrow, first, last, *refs):
    if first:
        recv_ref, part_ref, other_ref, src_ref, back_ref, half_ref, index_ref, right, left = refs
    elif last:
        recv_ref, index_ref, right, src_ref, left = refs
    else:
        recv_ref, part_ref, other_ref, index_ref, right = refs[:5]
        src_ref, back_ref, half_ref, known_ref, left = refs[5:]
    if not last:
        half_ref[...] = part_ref[...] + other_ref[...]
    tiles, cap = index_ref.shape[0], recv_ref.shape[2]
    per = cap // LANE
    levels = SRC_DEV // HIGH
    keep = row_iota(8) < 5
    if first:
        for t in range(tiles):
            index_ref[t : t + 1, :] = entry(recv_ref, per, t)[5:6].astype(I32)
        mark_high(right, index_ref[...])
    elif not last:
        known = recv_ref[0, :, 0:LANE]
        for n in range(1, narrow):
            known = known + recv_ref[n, :, 0:LANE]
        known_ref[...] = known
    for t in range(tiles):
        here = index_ref[t : t + 1, :]
        values = jnp.where(keep, entry(recv_ref, per, t), 0.0)
        spread_rows(left, values, here // HIGH, t * LANE, levels)
    sums = jnp.dot(left[...], right[...], preferred_element_type=F32)
    size = 8 * levels
    sums = sums[:size] + (sums[size : 2 * size] + sums[2 * size :])
    for level in range(levels):
        src_ref[:, level * HIGH : (level + 1) * HIGH] = sums[level * 8 : (level + 1) * 8]
    if last:
        return
    square = jnp.sum(src_ref[...] * src_ref[...]) if first else 0.0
    mark = jnp.where((row_iota(8) == 6) & (lane_iota(8) == 0), square, 0.0)
    for t in range(tiles):
        values = pick(
            lambda c: src_ref[:, c * LANE : (c + 1) * LANE],
            SRC_DEV // LANE,
            index_ref[t : t + 1, :],
        )
        values = jnp.where(keep, values, mark)
        back_ref[t // per, :, (t % per) * LANE : (t % per + 1) * LANE] = values


def lane_value(row, at):
    return jnp.sum(jnp.where(lane_iota(1) == at, row, 0.0), axis=1, keepdims=True)


def product_kernel(
    narrow, first, recv_ref, half_ref, later_ref, known_ref, pos_ref, seg_ref, order_ref, right,
    table_ref, full_ref, att_ref, sent_ref, scale_ref, vec, blocks, left, *own,
):
    send_ref = sent_ref if first else own[0]
    tiles, rows = pos_ref.shape[0], table_ref.shape[1]
    per = recv_ref.shape[2] // LANE
    full = half_ref[...] + later_ref[...]
    full_ref[...] = full[:, :SEG_DEV]
    notes = full[0:1, SEG_DEV:]
    lane, row = lane_iota(8), row_iota(8)
    send_note = jnp.zeros((8, LANE), F32)
    att_note = jnp.zeros((16, LANE), F32)
    if first:
        scale = jnp.ones((1, 1), F32)
        square_src = recv_ref[0, 6:7, 0:LANE]
        for n in range(1, narrow):
            square_src = square_src + recv_ref[n, 6:7, 0:LANE]
        att_note = jnp.where(lane_iota(16) == 1, lane_value(square_src, 0), 0.0)
        square_att = jnp.sum(full[:, :SEG_DEV] * full[:, :SEG_DEV], keepdims=True)
        send_note = jnp.where(lane == 0, lane_value(notes, 0), 0.0)
        send_note = jnp.where(lane == 1, square_att, send_note)
        send_note = jnp.where(row == 6, send_note, 0.0)
    else:
        known = known_ref[6:7, :]
        square = lane_value(notes, 1) + lane_value(known, 1)
        scale = lane_value(known, 0) / square
    scale_ref[...] = jnp.broadcast_to(scale, (8, LANE))
    att_ref[:, SEG_DEV:] = att_note

    def gather(t):
        where_att = seg_ref[pl.ds(t, 1), :]
        for top in range(0, 24, 8):
            if top < 16:
                picked = pick(
                    lambda c: full_ref[top : top + 8, c * LANE : (c + 1) * LANE],
                    SEG_DEV // LANE,
                    where_att,
                )
            else:
                picked = pick(lambda c: entry(recv_ref, per, c), tiles, pos_ref[pl.ds(t, 1), :])
            vec[t, top : top + 8, :] = picked if first else picked * scale

    def multiply(t, carry):
        fill_att(blocks, seg_ref, left, jnp.maximum(t - 1, 0))
        image = None
        for i in range(rows):
            part = table_ref[t, i] * vec[t, i : i + 1, :]
            image = part if image is None else image + part
        for i in range(rows):
            blocks[t, i : i + 1, :] = jnp.sum(table_ref[t, i] * image, axis=0, keepdims=True)
        blocks[t, rows:24, :] = jnp.zeros((24 - rows, LANE), F32)
        gather(jnp.minimum(t + 1, tiles - 1))
        return carry

    gather(0)
    lax.fori_loop(0, tiles, multiply, 0)
    send_sorted(narrow, blocks, order_ref, lambda t: send_note, send_ref)
    if not first:
        sending = pltpu.make_async_copy(send_ref, sent_ref, own[1])
        sending.start()
    fill_att(blocks, seg_ref, left, tiles - 1)
    scatter_att(att_ref, left, right)
    if not first:
        sending.wait()


def dots_kernel(
    src0, src1, src2, att0, att1, mine, later, square_ref, scale_ref, side_ref, out_ref, kept_ref
):
    kept_ref[...] = mine[...] + later[...]
    scale = scale_ref[0:1, 0:1]
    upper, weight = side_ref[0:1, 0:1] > 0.5, side_ref[1:2, 0:1]
    half = kept_ref.shape[1]

    def own_half(ref):
        return jnp.where(upper, ref[:, half:], ref[:, :half])

    src = (src0[...], src1[...] * scale, src2[...] * scale)
    att = (own_half(att0), own_half(att1) * scale, kept_ref[...] * scale)
    out = jnp.where(lane_iota(1) == 0, jnp.sum(square_ref[...], keepdims=True), 0.0)
    for at, (one, two) in enumerate(((0, 0), (0, 1), (1, 1), (1, 2), (2, 2))):
        total = jnp.sum(src[one] * src[two], keepdims=True)
        total = total + weight * jnp.sum(att[one] * att[two], keepdims=True)
        out = jnp.where(lane_iota(1) == at + 1, total, out)
    out_ref[...] = jnp.broadcast_to(out, out_ref.shape)


def finish_kernel(
    dots_ref, scale_ref, side_ref, src0, src1, src2, att0, att1, kept, other, rest,
    sol_src, sol_att, dir_src, dir_att, att2,
):
    upper = side_ref[0:1, 0:1] > 0.5
    half = kept.shape[1]
    dropped = other[...] + rest[...]
    att2[:, :half] = jnp.where(upper, dropped, kept[...])
    att2[:, half:] = jnp.where(upper, kept[...], dropped)
    sums = jnp.sum(dots_ref[...], axis=0, keepdims=True)
    rhs_square, m0, m1, m2, m3, m4 = [lane_value(sums, at) for at in range(6)]
    scale = scale_ref[0:1, 0:1]
    mean = m1 / m0
    ww = m2 - mean * m1
    wz = m3 - 2.0 * mean * m2 + mean * mean * m1
    zz = m4 - 2.0 * mean * m3 + mean * mean * m2
    root0, root1 = jnp.sqrt(m0), jnp.sqrt(ww)
    beta1 = jnp.sqrt(rhs_square)
    alpha1 = root0 / beta1
    beta2 = jnp.sqrt(mean / scale - alpha1 * alpha1)
    cross = root1 / (scale * root0)
    alpha2 = cross / beta2
    quotient = wz / ww / scale
    beta3 = jnp.sqrt(quotient - alpha2 * alpha2)
    third = zz / ww / (scale * scale) - quotient * quotient - cross * cross
    alpha3 = jnp.sqrt(third) / beta3
    phi_bar, rho_bar = beta1, alpha1
    steps, turns = [], []
    for beta, alpha in ((beta2, alpha2), (beta3, alpha3)):
        rho = jnp.sqrt(rho_bar * rho_bar + beta * beta)
        cosine, sine = rho_bar / rho, beta / rho
        theta = sine * alpha
        rho_bar = -cosine * alpha
        steps.append(cosine * phi_bar / rho)
        turns.append(theta / rho)
        phi_bar = sine * phi_bar
    sides = (
        (src0, src1, src2, sol_src, dir_src),
        (att0, att1, att2, sol_att, dir_att),
    )
    for zero, one, two, sol, direction in sides:
        rows = sol.shape[0]
        base, once, twice = zero[0:rows], one[0:rows] * scale, two[0:rows] * scale
        v1 = base / root0
        v2 = (once - mean * base) / root1
        v3 = ((twice - mean * once) / (scale * root1) - quotient * v2 - cross * v1) / (
            beta3 * alpha3
        )
        turned = v2 - turns[0] * v1
        sol[...] = steps[0] * v1 + steps[1] * turned
        direction[...] = v3 - turns[1] * turned


def sds(shape, dtype=F32):
    return jax.ShapeDtypeStruct(shape, dtype)


def in_hbm(values):
    return pltpu.with_memory_space_constraint(values, pltpu.HBM)


def call(kernel, outs, scratch=(), limit=8, **more):
    return pl.pallas_call(
        kernel,
        out_shape=outs,
        scratch_shapes=list(scratch),
        compiler_params=pltpu.CompilerParams(vmem_limit_bytes=limit * MIB),
        **more,
    )


def on_device(src_design, att_design, right_side, block_source, block_segment, block_count):
    narrow, wide = lax.axis_size("narrow"), lax.axis_size("wide")
    devices = narrow * wide
    blocks = block_source.shape[0]
    tiles = blocks // LANE
    cap = blocks // narrow
    src_rows, att_rows = src_design.shape[0], att_design.shape[0]
    rows = src_rows + att_rows
    columns = right_side.shape[0] // LANE
    groups = columns // LANE
    obs = right_side.shape[0] // blocks

    def across(values, step):
        return lax.ppermute(values, "wide", [(i, i ^ step) for i in range(wide)])

    def exchange(values):
        return lax.all_to_all(values, "narrow", 0, 0)

    def far_sums(total, end):
        later, jump = None, 2
        while jump < end:
            if later is not None:
                total = total + later
            later = across(total, jump)
            jump *= 2
        return total, later

    upper = lax.axis_index("wide") >= wide // 2

    tile_rows = lambda values: values.reshape(tiles, LANE)
    att_view = att_design.reshape(att_rows // 8, 8, columns, LANE).transpose(0, 2, 1, 3)
    src_view = src_design.reshape(src_rows, columns, LANE).transpose(1, 0, 2)

    right_shape = sds((blocks, HIGH), BF16)
    att_left = pltpu.VMEM((3 * 16 * SEG_DEV // HIGH, blocks), BF16)
    src_left = pltpu.VMEM((3 * 8 * SRC_DEV // HIGH, blocks), BF16)
    tile_int = sds((tiles, LANE), I32)
    send_shape = sds((narrow, 8, cap))
    att_shape = sds((16, SEG_DEV + LANE))
    src_shape = sds((8, SRC_DEV))
    table_shape = (tiles, rows, obs, LANE)
    table, square, pos, seg, order, att_right, part, send = call(
        functools.partial(start_kernel, narrow),
        (
            sds(table_shape),
            sds((8, LANE)),
            tile_int,
            tile_int,
            tile_int,
            right_shape,
            att_shape,
            send_shape,
        ),
        [
            pltpu.VMEM((groups, att_rows // 8, LANE, 8, LANE), F32),
            pltpu.VMEM((groups, LANE, 8, LANE), F32),
            pltpu.VMEM((groups, LANE, LANE), F32),
            pltpu.VMEM((tiles, LANE), I32),
            pltpu.VMEM((tiles, LANE), I32),
            pltpu.VMEM((tiles, LANE), I32),
            pltpu.VMEM((tiles, 24, LANE), F32),
            pltpu.VMEM((tiles, LANE), F32),
            pltpu.VMEM((2, 24 * 8, LANE), F32),
            pltpu.VMEM((LANE, 3 * LANE), BF16),
            att_left,
            pltpu.SemaphoreType.DMA((3, groups)),
            pltpu.SemaphoreType.DMA((3,)),
        ],
        in_specs=[pl.BlockSpec(memory_space=pltpu.HBM)] * 6,
        limit=20,
    )(
        *map(
            in_hbm,
            (
                att_view,
                src_view,
                right_side.reshape(columns, LANE),
                tile_rows(block_source),
                tile_rows(block_segment),
                tile_rows(block_count),
            ),
        )
    )

    results = []
    note = jnp.zeros((8, LANE), F32)
    owners = None
    for step in range(3):
        first_time, last_time = step == 0, step == 2
        other = across(part, 1)
        arrived = exchange(send)
        kernel = functools.partial(owner_kernel, narrow, first_time, last_time)
        if last_time:
            total, later = far_sums(part + other, wide // 2)
            if later is not None:
                total = total + later
            low, high = total[:, : SEG_DEV // 2], total[:, SEG_DEV // 2 : SEG_DEV]
            mine, other = jnp.where(upper, high, low), jnp.where(upper, low, high)
            later = across(other, wide // 2)
            rest = across(mine, wide // 2)
            src_sum = call(kernel, src_shape, [src_left])(arrived, *owners)
            results.append((src_sum, mine, later))
            break
        outs = (src_shape, send_shape, att_shape)
        if first_time:
            src_sum, back, half, *owners = call(
                kernel, outs + (tile_int, right_shape), [src_left]
            )(arrived, part, other)
        else:
            src_sum, back, half, note = call(kernel, outs + (sds((8, LANE)),), [src_left])(
                arrived, part, other, *owners
            )
        total, later = far_sums(half, wide)
        back = exchange(back)
        own, specs = [], {}
        if not first_time:
            in_vmem = pl.BlockSpec(memory_space=pltpu.VMEM)
            own = [pltpu.VMEM(send_shape.shape, F32), pltpu.SemaphoreType.DMA(())]
            specs = dict(
                out_specs=(in_vmem, in_vmem, pl.BlockSpec(memory_space=pltpu.HBM), in_vmem)
            )
        att_sum, part, send, scale = call(
            functools.partial(product_kernel, narrow, first_time),
            (
                sds((16, SEG_DEV)),
                att_shape,
                send_shape if first_time else pltpu.HBM(send_shape.shape, F32),
                sds((8, LANE)),
            ),
            [
                pltpu.VMEM((tiles, 24, LANE), F32),
                pltpu.VMEM((tiles, 24, LANE), F32),
                att_left,
            ]
            + own,
            **specs,
        )(back, total, later, note, pos, seg, order, att_right, table)
        results.append((src_sum, att_sum))
    counted = lax.axis_index("wide") % (wide // 2) == 0
    side = jnp.where(row_iota(8) == 0, upper, counted).astype(F32)
    (src0, att0), (src1, att1), (src2, mine, later) = results
    dots, kept = call(dots_kernel, (sds((devices, LANE)), sds((16, SEG_DEV // 2))))(
        src0, src1, src2, att0, att1, mine, later, square, scale, side
    )
    dots = lax.all_to_all(dots, ("wide", "narrow"), 0, 0, tiled=True)
    sol_src, sol_att, dir_src, dir_att = call(
        finish_kernel,
        (
            sds((src_rows, SRC_DEV)),
            sds((att_rows, SEG_DEV)),
            sds((src_rows, SRC_DEV)),
            sds((att_rows, SEG_DEV)),
        ),
        [pltpu.VMEM((16, SEG_DEV), F32)],
    )(dots, scale, side, src0, src1, src2, att0, att1, kept, other, rest)
    return (sol_src, sol_att, dir_src, dir_att)


def solution(mesh):
    both = ("wide", "narrow")
    in_specs = (P(None, both), P(None, both), P(both), P(both), P(both), P(both))
    out_specs = (P(None, both), P(None, "narrow"), P(None, both), P(None, "narrow"))

    return jax.shard_map(
        on_device, mesh=mesh, in_specs=in_specs, out_specs=out_specs, check_vma=False
    )
```

profile of v0, /device:TPU:0, one launch (start us, length us, event | category | flops | bytes accessed | tf_op | source)
XLA Modules:
  0.0 80.7 jit_solution(11665747461582592953)
XLA Ops:
  0.6 5.9 %shard_map.93 = (f32[16,21,64,128]{3,2,1,0:T(8,128)S(1)}, f32[8,128]{1,0:T(8,128)S(1)}, s32[16,128]{1,0:T(8,128)S(1)}, s32[16,128]{1,0:T(8,128)S(1)}, s32[16,128...) custom-call(f32[2,1024,8,128]{3,2,1,0:T(8,128)} %bitcast.15, ...), custom_call_target="tpu_custom_call" | custom-call | tf_op jit(solution)/shard_map/pallas_call | solution.py:537
  6.6 3.1 %collective-permute-start = (f32[16,1152]{1,0:T(8,128)S(1)}, f32[16,1152]{1,0:T(8,128)S(1)}, u32[]{:S(2)}, u32[]{:S(2)}) collective-permute-start(f32[16,1152]{1,0:T(8,128)S(1)} %get-tuple-element.31.refs_1_), channel_id=1, source_target_pairs={{0,8},{8,0},{16,24},{24,16},{1,9},{9,1},{17,25},{25,17},{2,10},{10... | collective-permute-start | bytes 221192 | tf_op jit(solution)/shard_map/ppermute | solution.py:509
  9.7 8.5 %all_to_all.36.refs_0_ = f32[8,8,256]{2,1,0:T(8,128)S(1)} all-to-all(f32[8,8,256]{2,1,0:T(8,128)S(1)} %get-tuple-element.30), channel_id=1, replica_groups=mesh['wide'=4,'narrow'=8] {'narrow'}, dimensions={0} | all-to-all | bytes 131072 | tf_op jit(solution)/shard_map/all_to_all | solution.py:512
  18.2 1.4 %shard_map.94 = (f32[8,2048]{1,0:T(8,128)S(1)}, f32[8,8,256]{2,1,0:T(8,128)S(1)}, f32[16,1152]{1,0:T(8,128)S(1)}, s32[16,128]{1,0:T(8,128)S(1)}, bf16[2048,256]{1,0:T(8,128)(2,1)S(1)}) custom-call(f32[8,8,256]{2,1,0:T(8,128)S(1)} %all_to_all.36.refs_0_, f32[16,1152]{1,0:T(8,128)S(1)} %get-tuple-element.31.refs_1_, f32[16,1152]{1,0:T(8,128)S(1)} %collective-permute-done.refs_2_), custom_call_target="tpu_custom_call" | custom-call | tf_op jit(solution)/shard_map/pallas_call | solution.py:601
  19.6 2.7 %collective-permute-start.1 = (f32[16,1152]{1,0:T(8,128)S(1)}, f32[16,1152]{1,0:T(8,128)S(1)}, u32[]{:S(2)}, u32[]{:S(2)}) collective-permute-start(f32[16,1152]{1,0:T(8,128)S(1)} %get-tuple-element.34.half_ref), channel_id=1, source_target_pairs={{0,16},{8,24},{16,0},{24,8},{1,17},{9,25},{17,1},{25,9},{2,18},{10... | collective-permute-start | bytes 221192 | tf_op jit(solution)/shard_map/ppermute | solution.py:509
  22.3 7.4 %all_to_all.37.recv_ref = f32[8,8,256]{2,1,0:T(8,128)S(1)} all-to-all(f32[8,8,256]{2,1,0:T(8,128)S(1)} %get-tuple-element.33), channel_id=1, replica_groups=mesh['wide'=4,'narrow'=8] {'narrow'}, dimensions={0} | all-to-all | bytes 131072 | tf_op jit(solution)/shard_map/all_to_all | solution.py:512
  29.7 4.2 %shard_map.95 = (f32[16,1024]{1,0:T(8,128)S(1)}, f32[16,1152]{1,0:T(8,128)S(1)}, f32[8,8,256]{2,1,0:T(8,128)S(1)}, f32[8,128]{1,0:T(8,128)}) custom-call(f32[8,8,256]{2,1,0:T(8,128)S(1)} %all_to_all.37.recv_ref, f32[16,1152]{1,0:T(8,128)S(1)} %get-tuple-element.34.half_ref, f32[16,1152]{1,0:T(8,128)S(1)} %collective-permute-done.1.later_ref, ...), custom_call_target="tpu_custom_call" | custom-call | tf_op jit(solution)/shard_map/pallas_call | solution.py:617
  33.8 0.4 collective-permute-start.2
  34.3 7.4 %all_to_all.38.refs_0_ = f32[8,8,256]{2,1,0:T(8,128)S(1)} all-to-all(f32[8,8,256]{2,1,0:T(8,128)S(1)} %get-tuple-element.40), channel_id=1, replica_groups=mesh['wide'=4,'narrow'=8] {'narrow'}, dimensions={0} | all-to-all | bytes 131072 | tf_op jit(solution)/shard_map/all_to_all | solution.py:512
  41.7 1.1 %shard_map.96 = (f32[8,2048]{1,0:T(8,128)S(1)}, f32[8,8,256]{2,1,0:T(8,128)S(1)}, f32[16,1152]{1,0:T(8,128)S(1)}, f32[8,128]{1,0:T(8,128)S(1)}) custom-call(f32[8,8,256]{2,1,0:T(8,128)S(1)} %all_to_all.38.refs_0_, f32[16,1152]{1,0:T(8,128)S(1)} %get-tuple-element.41.refs_1_, f32[16,1152]{1,0:T(8,128)S(1)} %collective-permute-done.2.refs_2_, ...), custom_call_target="tpu_custom_call" | custom-call | tf_op jit(solution)/shard_map/pallas_call | solution.py:605
  42.7 0.4 collective-permute-start.3
  43.1 7.4 %all_to_all.39.recv_ref = f32[8,8,256]{2,1,0:T(8,128)S(1)} all-to-all(f32[8,8,256]{2,1,0:T(8,128)S(1)} %get-tuple-element.45), channel_id=1, replica_groups=mesh['wide'=4,'narrow'=8] {'narrow'}, dimensions={0} | all-to-all | bytes 131072 | tf_op jit(solution)/shard_map/all_to_all | solution.py:512
  50.5 4.7 %shard_map.97 = (f32[16,1024]{1,0:T(8,128)S(1)}, f32[16,1152]{1,0:T(8,128)S(1)}, f32[8,8,256]{2,1,0:T(8,128)}, f32[8,128]{1,0:T(8,128)S(1)}) custom-call(f32[8,8,256]{2,1,0:T(8,128)S(1)} %all_to_all.39.recv_ref, f32[16,1152]{1,0:T(8,128)S(1)} %get-tuple-element.46.half_ref, f32[16,1152]{1,0:T(8,128)S(1)} %collective-permute-done.3.later_ref, ...), custom_call_target="tpu_custom_call" | custom-call | tf_op jit(solution)/shard_map/pallas_call | solution.py:617
  55.3 1.6 %collective-permute-start.4 = (f32[16,1152]{1,0:T(8,128)S(1)}, f32[16,1152]{1,0:T(8,128)S(1)}, u32[]{:S(2)}, u32[]{:S(2)}) collective-permute-start(f32[16,1152]{1,0:T(8,128)S(1)} %get-tuple-element.51), channel_id=1, source_target_pairs={{0,8},{8,0},{16,24},{24,16},{1,9},{9,1},{17,25},{25,17},{2,10},{10... | collective-permute-start | bytes 221192 | tf_op jit(solution)/shard_map/ppermute | solution.py:509
  56.9 3.4 %all-to-all-start.4 = ((f32[8,8,256]{2,1,0:T(8,128)}), f32[8,8,256]{2,1,0:T(8,128)S(1)}, u32[]{:S(2)}, u32[]{:S(2)}) async-start(f32[8,8,256]{2,1,0:T(8,128)} %get-tuple-element.48), calls=%async_computation.4 | async-start | bytes 131072 | tf_op jit(solution)/shard_map/all_to_all | solution.py:512
  60.3 2.7 %collective-permute-start.5 = (f32[16,512]{1,0:T(8,128)S(1)}, f32[16,512]{1,0:T(8,128)S(1)}, u32[]{:S(2)}, u32[]{:S(2)}) collective-permute-start(f32[16,512]{1,0:T(8,128)S(1)} %get-tuple-element.56.other), channel_id=1, source_target_pairs={{0,16},{8,24},{16,0},{24,8},{1,17},{9,25},{17,1},{25,9},{2,18},{10... | collective-permute-start | bytes 98312 | tf_op jit(solution)/shard_map/ppermute | solution.py:509
  63.0 0.3 collective-permute-start.6
  63.3 1.9 %all-to-all-done.4.refs_0_ = f32[8,8,256]{2,1,0:T(8,128)S(1)} async-done(((f32[8,8,256]{2,1,0:T(8,128)}), f32[8,8,256]{2,1,0:T(8,128)S(1)}, u32[]{:S(2)}, u32[]{:S(2)}) %all-to-all-start.4) | async-done | bytes 65568 | tf_op jit(solution)/shard_map/all_to_all | solution.py:512
  65.2 0.4 shard_map.98.src2
  65.7 0.1 iota.7.side_ref
  65.7 0.9 %shard_map.99 = (f32[32,128]{1,0:T(8,128)}, f32[16,512]{1,0:T(8,128)S(1)}) custom-call(f32[8,2048]{1,0:T(8,128)S(1)} %get-tuple-element.32.src0, f32[8,2048]{1,0:T(8,128)S(1)} %get-tuple-element.44.src1, f32[8,2048]{1,0:T(8,128)S(1)} %shard_map.98.src2, f32[16,1024]{1,0:T(8,128)S(1)} %get-tuple-element.49.att0, f32[16,1024]{1,0:T(8,128)S(1)} %get-tuple-element.50.att1, ...), custom_call_target="tpu_custom_call" | custom-call | tf_op jit(solution)/shard_map/pallas_call | solution.py:637
  66.6 6.1 %all-to-all-start.5 = ((f32[32,1,128]{2,1,0:T(1,128)}), f32[32,1,128]{2,1,0:T(1,128)S(1)}, u32[]{:S(2)}, u32[]{:S(2)}) async-start(f32[32,1,128]{2,1,0:T(1,128)} %bitcast.9), calls=%async_computation.5 | async-start | bytes 32768 | tf_op jit(solution)/shard_map/all_to_all | solution.py:640
  72.7 7.1 %all-to-all-done.5 = f32[32,1,128]{2,1,0:T(1,128)S(1)} async-done(((f32[32,1,128]{2,1,0:T(1,128)}), f32[32,1,128]{2,1,0:T(1,128)S(1)}, u32[]{:S(2)}, u32[]{:S(2)}) %all-to-all-start.5) | async-done | bytes 16416 | tf_op jit(solution)/shard_map/all_to_all | solution.py:640
  79.8 0.9 %shard_map.100 = (f32[5,2048]{1,0:T(8,128)}, f32[16,1024]{1,0:T(8,128)}, f32[5,2048]{1,0:T(8,128)}, f32[16,1024]{1,0:T(8,128)}) custom-call(f32[32,128]{1,0:T(8,128)S(1)} %bitcast.14, f32[8,128]{1,0:T(8,128)S(1)} %get-tuple-element.53.scale_ref, f32[8,128]{1,0:T(8,128)S(1)} %iota.7.side_ref, f32[8,2048]{1,0:T(8,128)S(1)} %get-tuple-element.32.src0, ...), custom_call_target="tpu_custom_call" | custom-call | tf_op jit(solution)/shard_map/pallas_call | solution.py:641
  (11 shorter events, 0.0 us)
Async XLA Ops:
  6.6 11.6 %collective-permute-start = (f32[16,1152]{1,0:T(8,128)S(1)}, f32[16,1152]{1,0:T(8,128)S(1)}, u32[]{:S(2)}, u32[]{:S(2)}) collective-permute-start(f32[16,1152]{1,0:T(8,128)S(1)} %get-tuple-element.31.refs_1_), channel_id=1, source_target_pairs={{0,8},{8,0},{16,24},{24,16},{1,9},{9,1},{17,25},{25,17},{2,10},{10... | collective-permute-start | bytes 221192 | tf_op jit(solution)/shard_map/ppermute | solution.py:509
  19.6 10.0 %collective-permute-start.1 = (f32[16,1152]{1,0:T(8,128)S(1)}, f32[16,1152]{1,0:T(8,128)S(1)}, u32[]{:S(2)}, u32[]{:S(2)}) collective-permute-start(f32[16,1152]{1,0:T(8,128)S(1)} %get-tuple-element.34.half_ref), channel_id=1, source_target_pairs={{0,16},{8,24},{16,0},{24,8},{1,17},{9,25},{17,1},{25,9},{2,18},{10... | collective-permute-start | bytes 221192 | tf_op jit(solution)/shard_map/ppermute | solution.py:509
  33.8 7.8 %collective-permute-start.2 = (f32[16,1152]{1,0:T(8,128)S(1)}, f32[16,1152]{1,0:T(8,128)S(1)}, u32[]{:S(2)}, u32[]{:S(2)}) collective-permute-start(f32[16,1152]{1,0:T(8,128)S(1)} %get-tuple-element.41.refs_1_), channel_id=1, source_target_pairs={{0,8},{8,0},{16,24},{24,16},{1,9},{9,1},{17,25},{25,17},{2,10},{10... | collective-permute-start | bytes 221192 | tf_op jit(solution)/shard_map/ppermute | solution.py:509
  42.7 7.8 %collective-permute-start.3 = (f32[16,1152]{1,0:T(8,128)S(1)}, f32[16,1152]{1,0:T(8,128)S(1)}, u32[]{:S(2)}, u32[]{:S(2)}) collective-permute-start(f32[16,1152]{1,0:T(8,128)S(1)} %get-tuple-element.46.half_ref), channel_id=1, source_target_pairs={{0,16},{8,24},{16,0},{24,8},{1,17},{9,25},{17,1},{25,9},{2,18},{10... | collective-permute-start | bytes 221192 | tf_op jit(solution)/shard_map/ppermute | solution.py:509
  55.3 5.0 %collective-permute-start.4 = (f32[16,1152]{1,0:T(8,128)S(1)}, f32[16,1152]{1,0:T(8,128)S(1)}, u32[]{:S(2)}, u32[]{:S(2)}) collective-permute-start(f32[16,1152]{1,0:T(8,128)S(1)} %get-tuple-element.51), channel_id=1, source_target_pairs={{0,8},{8,0},{16,24},{24,16},{1,9},{9,1},{17,25},{25,17},{2,10},{10... | collective-permute-start | bytes 221192 | tf_op jit(solution)/shard_map/ppermute | solution.py:509
  56.9 8.3 %all-to-all-start.4 = ((f32[8,8,256]{2,1,0:T(8,128)}), f32[8,8,256]{2,1,0:T(8,128)S(1)}, u32[]{:S(2)}, u32[]{:S(2)}) async-start(f32[8,8,256]{2,1,0:T(8,128)} %get-tuple-element.48), calls=%async_computation.4 | async-start | bytes 131072 | tf_op jit(solution)/shard_map/all_to_all | solution.py:512
  60.3 5.3 %collective-permute-start.5 = (f32[16,512]{1,0:T(8,128)S(1)}, f32[16,512]{1,0:T(8,128)S(1)}, u32[]{:S(2)}, u32[]{:S(2)}) collective-permute-start(f32[16,512]{1,0:T(8,128)S(1)} %get-tuple-element.56.other), channel_id=1, source_target_pairs={{0,16},{8,24},{16,0},{24,8},{1,17},{9,25},{17,1},{25,9},{2,18},{10... | collective-permute-start | bytes 98312 | tf_op jit(solution)/shard_map/ppermute | solution.py:509
  63.0 9.7 %collective-permute-start.6 = (f32[16,512]{1,0:T(8,128)S(1)}, f32[16,512]{1,0:T(8,128)S(1)}, u32[]{:S(2)}, u32[]{:S(2)}) collective-permute-start(f32[16,512]{1,0:T(8,128)S(1)} %get-tuple-element.57.mine), channel_id=1, source_target_pairs={{0,16},{8,24},{16,0},{24,8},{1,17},{9,25},{17,1},{25,9},{2,18},{10... | collective-permute-start | bytes 98312 | tf_op jit(solution)/shard_map/ppermute | solution.py:509
  66.6 13.2 %all-to-all-start.5 = ((f32[32,1,128]{2,1,0:T(1,128)}), f32[32,1,128]{2,1,0:T(1,128)S(1)}, u32[]{:S(2)}, u32[]{:S(2)}) async-start(f32[32,1,128]{2,1,0:T(1,128)} %bitcast.9), calls=%async_computation.5 | async-start | bytes 32768 | tf_op jit(solution)/shard_map/all_to_all | solution.py:640
where the time goes:
time: 81.2 us; the launch traced here: 80.7 us
  blocking collectives  30.7 us (38%)
  starting transfers between devices  20.7 us (25%)
  Pallas kernels  19.5 us (24%)
  waiting for transfers between devices  9.02 us (11%)
    all_to_all x4, blocking collectives, exchange(): return lax.all_to_all(values, 'narrow', 0, 0)  30.7 us
    ppermute x7, starting transfers between devices, across(): return lax.ppermute(values, 'wide', [(i, i ^ step) for i in range(wide)])  11.3 us
    pallas_call x2, Pallas kernels, on_device(): call(functools.partial(product_kernel, narrow, first_time), (sds((16, SEG...  8.89 us
    all_to_all x1, waiting for transfers between devices, on_device(): dots = lax.all_to_all(dots, ('wide', 'narrow'), 0, 0, tiled=True)  7.09 us
    all_to_all x1, starting transfers between devices, on_device(): dots = lax.all_to_all(dots, ('wide', 'narrow'), 0, 0, tiled=True)  6.06 us
    pallas_call x1, Pallas kernels, on_device(): call(functools.partial(start_kernel, narrow), (sds(table_shape), sds((8,...  5.92 us
    all_to_all x1, starting transfers between devices, exchange(): return lax.all_to_all(values, 'narrow', 0, 0)  3.35 us
    all_to_all x1, waiting for transfers between devices, exchange(): return lax.all_to_all(values, 'narrow', 0, 0)  1.91 us
  transfers between devices with their start and end apart: 9, of which 2 were waited for; matrix products, arithmetic and copies ran while one was open for 0% of the time, Pallas kernels for 2%

commit v1 on v0

--- a/solution.py
+++ b/solution.py
@@ -390,7 +390,7 @@
         return carry
 
     gather(0)
-    lax.fori_loop(0, tiles, multiply, 0)
+    lax.fori_loop(0, tiles, multiply, 0, unroll=4)
     send_sorted(narrow, blocks, order_ref, lambda t: send_note, send_ref)
     if not first:
         sending = pltpu.make_async_copy(send_ref, sent_ref, own[1])
@@ -423,14 +423,13 @@
 
 
 def finish_kernel(
-    dots_ref, scale_ref, side_ref, src0, src1, src2, att0, att1, kept, other, rest,
+    dots_ref, scale_ref, side_ref, src0, src1, src2, att0, att1, kept, back,
     sol_src, sol_att, dir_src, dir_att, att2,
 ):
     upper = side_ref[0:1, 0:1] > 0.5
     half = kept.shape[1]
-    dropped = other[...] + rest[...]
-    att2[:, :half] = jnp.where(upper, dropped, kept[...])
-    att2[:, half:] = jnp.where(upper, kept[...], dropped)
+    att2[:, :half] = jnp.where(upper, back[...], kept[...])
+    att2[:, half:] = jnp.where(upper, kept[...], back[...])
     sums = jnp.sum(dots_ref[...], axis=0, keepdims=True)
     rhs_square, m0, m1, m2, m3, m4 = [lane_value(sums, at) for at in range(6)]
     scale = scale_ref[0:1, 0:1]
@@ -592,7 +591,6 @@
             low, high = total[:, : SEG_DEV // 2], total[:, SEG_DEV // 2 : SEG_DEV]
             mine, other = jnp.where(upper, high, low), jnp.where(upper, low, high)
             later = across(other, wide // 2)
-            rest = across(mine, wide // 2)
             src_sum = call(kernel, src_shape, [src_left])(arrived, *owners)
             results.append((src_sum, mine, later))
             break
@@ -638,6 +636,7 @@
         src0, src1, src2, att0, att1, mine, later, square, scale, side
     )
     dots = lax.all_to_all(dots, ("wide", "narrow"), 0, 0, tiled=True)
+    back = across(kept, wide // 2)
     sol_src, sol_att, dir_src, dir_att = call(
         finish_kernel,
         (
@@ -647,7 +646,7 @@
             sds((att_rows, SEG_DEV)),
         ),
         [pltpu.VMEM((16, SEG_DEV), F32)],
-    )(dots, scale, side, src0, src1, src2, att0, att1, kept, other, rest)
+    )(dots, scale, side, src0, src1, src2, att0, att1, kept, back)
     return (sol_src, sol_att, dir_src, dir_att)
 
 

time: 81.2 us -> 77.7 us (0.957)
  blocking collectives: 30.7 us -> 40.6 us
  waiting for transfers between devices: 9.02 us -> 2.26 us
  starting transfers between devices: 20.7 us -> 16.9 us
  Pallas kernels: 19.5 us -> 16.7 us
    all_to_all x0 -> x1, blocking collectives: none -> 9.96 us  [on_device(): dots = lax.all_to_all(dots, ('wide', 'narrow'), 0, 0, tiled=True)]
    all_to_all x1 -> x0, waiting for transfers between devices: 7.09 us -> none  [on_device(): dots = lax.all_to_all(dots, ('wide', 'narrow'), 0, 0, tiled=True)]
    all_to_all x1 -> x0, starting transfers between devices: 6.06 us -> none  [on_device(): dots = lax.all_to_all(dots, ('wide', 'narrow'), 0, 0, tiled=True)]
    ppermute x7, starting transfers between devices: 11.3 us -> 13.6 us  [across(): return lax.ppermute(values, 'wide', [(i, i ^ step) for i in range(wide)])]
    pallas_call x2, Pallas kernels: 8.89 us -> 6.61 us  [on_device(): call(functools.partial(product_kernel, narrow, first_time), (sds((16, SEG...]
  transfers between devices with their start and end apart: 9 -> 8, of which waited for: 2 -> 1; matrix products, arithmetic and copies ran while one was open for 0% -> 0% of each run, Pallas kernels for 2% -> 1%
where the time goes in v1:
time: 77.7 us; the launch traced here: 77.3 us
  blocking collectives  40.6 us (52%)
  starting transfers between devices  16.9 us (22%)
  Pallas kernels  16.7 us (21%)
  waiting for transfers between devices  2.26 us (3%)
    all_to_all x4, blocking collectives, exchange(): return lax.all_to_all(values, 'narrow', 0, 0)  30.7 us
    ppermute x7, starting transfers between devices, across(): return lax.ppermute(values, 'wide', [(i, i ^ step) for i in range(wide)])  13.6 us
    all_to_all x1, blocking collectives, on_device(): dots = lax.all_to_all(dots, ('wide', 'narrow'), 0, 0, tiled=True)  9.96 us
    pallas_call x2, Pallas kernels, on_device(): call(functools.partial(product_kernel, narrow, first_time), (sds((16, SEG...  6.61 us
    pallas_call x1, Pallas kernels, on_device(): call(functools.partial(start_kernel, narrow), (sds(table_shape), sds((8,...  5.95 us
    all_to_all x1, starting transfers between devices, exchange(): return lax.all_to_all(values, 'narrow', 0, 0)  3.35 us
    all_to_all x1, waiting for transfers between devices, exchange(): return lax.all_to_all(values, 'narrow', 0, 0)  2.24 us
  transfers between devices with their start and end apart: 8, of which 1 were waited for; matrix products, arithmetic and copies ran while one was open for 0% of the time, Pallas kernels for 1%

profile of v1, /device:TPU:0, one launch (start us, length us, event | category | flops | bytes accessed | tf_op | source)
XLA Modules:
  0.0 77.3 jit_solution(6643534051586239235)
XLA Ops:
  0.6 5.9 %shard_map.93 = (f32[16,21,64,128]{3,2,1,0:T(8,128)S(1)}, f32[8,128]{1,0:T(8,128)S(1)}, s32[16,128]{1,0:T(8,128)S(1)}, s32[16,128]{1,0:T(8,128)S(1)}, s32[16,128...) custom-call(f32[2,1024,8,128]{3,2,1,0:T(8,128)} %bitcast.16, ...), custom_call_target="tpu_custom_call" | custom-call | tf_op jit(solution)/shard_map/pallas_call | solution.py:536
  6.6 3.1 %collective-permute-start = (f32[16,1152]{1,0:T(8,128)S(1)}, f32[16,1152]{1,0:T(8,128)S(1)}, u32[]{:S(2)}, u32[]{:S(2)}) collective-permute-start(f32[16,1152]{1,0:T(8,128)S(1)} %get-tuple-element.31.refs_1_), channel_id=1, source_target_pairs={{0,8},{8,0},{16,24},{24,16},{1,9},{9,1},{17,25},{25,17},{2,10},{10... | collective-permute-start | bytes 221192 | tf_op jit(solution)/shard_map/ppermute | solution.py:508
  9.7 8.5 %all_to_all.36.refs_0_ = f32[8,8,256]{2,1,0:T(8,128)S(1)} all-to-all(f32[8,8,256]{2,1,0:T(8,128)S(1)} %get-tuple-element.30), channel_id=1, replica_groups=mesh['wide'=4,'narrow'=8] {'narrow'}, dimensions={0} | all-to-all | bytes 131072 | tf_op jit(solution)/shard_map/all_to_all | solution.py:511
  18.2 1.4 %shard_map.94 = (f32[8,2048]{1,0:T(8,128)S(1)}, f32[8,8,256]{2,1,0:T(8,128)S(1)}, f32[16,1152]{1,0:T(8,128)S(1)}, s32[16,128]{1,0:T(8,128)S(1)}, bf16[2048,256]{1,0:T(8,128)(2,1)S(1)}) custom-call(f32[8,8,256]{2,1,0:T(8,128)S(1)} %all_to_all.36.refs_0_, f32[16,1152]{1,0:T(8,128)S(1)} %get-tuple-element.31.refs_1_, f32[16,1152]{1,0:T(8,128)S(1)} %collective-permute-done.refs_2_), custom_call_target="tpu_custom_call" | custom-call | tf_op jit(solution)/shard_map/pallas_call | solution.py:599
  19.7 2.7 %collective-permute-start.1 = (f32[16,1152]{1,0:T(8,128)S(1)}, f32[16,1152]{1,0:T(8,128)S(1)}, u32[]{:S(2)}, u32[]{:S(2)}) collective-permute-start(f32[16,1152]{1,0:T(8,128)S(1)} %get-tuple-element.34.half_ref), channel_id=1, source_target_pairs={{0,16},{8,24},{16,0},{24,8},{1,17},{9,25},{17,1},{25,9},{2,18},{10... | collective-permute-start | bytes 221192 | tf_op jit(solution)/shard_map/ppermute | solution.py:508
  22.3 7.4 %all_to_all.37.recv_ref = f32[8,8,256]{2,1,0:T(8,128)S(1)} all-to-all(f32[8,8,256]{2,1,0:T(8,128)S(1)} %get-tuple-element.33), channel_id=1, replica_groups=mesh['wide'=4,'narrow'=8] {'narrow'}, dimensions={0} | all-to-all | bytes 131072 | tf_op jit(solution)/shard_map/all_to_all | solution.py:511
  29.7 0.0 collective-permute-done.1.later_ref
  29.7 2.9 %shard_map.95 = (f32[16,1024]{1,0:T(8,128)S(1)}, f32[16,1152]{1,0:T(8,128)S(1)}, f32[8,8,256]{2,1,0:T(8,128)S(1)}, f32[8,128]{1,0:T(8,128)}) custom-call(f32[8,8,256]{2,1,0:T(8,128)S(1)} %all_to_all.37.recv_ref, f32[16,1152]{1,0:T(8,128)S(1)} %get-tuple-element.34.half_ref, f32[16,1152]{1,0:T(8,128)S(1)} %collective-permute-done.1.later_ref, ...), custom_call_target="tpu_custom_call" | custom-call | tf_op jit(solution)/shard_map/pallas_call | solution.py:615
  32.6 0.5 collective-permute-start.2
  33.1 7.4 %all_to_all.38.refs_0_ = f32[8,8,256]{2,1,0:T(8,128)S(1)} all-to-all(f32[8,8,256]{2,1,0:T(8,128)S(1)} %get-tuple-element.40), channel_id=1, replica_groups=mesh['wide'=4,'narrow'=8] {'narrow'}, dimensions={0} | all-to-all | bytes 131072 | tf_op jit(solution)/shard_map/all_to_all | solution.py:511
  40.5 1.1 %shard_map.96 = (f32[8,2048]{1,0:T(8,128)S(1)}, f32[8,8,256]{2,1,0:T(8,128)S(1)}, f32[16,1152]{1,0:T(8,128)S(1)}, f32[8,128]{1,0:T(8,128)S(1)}) custom-call(f32[8,8,256]{2,1,0:T(8,128)S(1)} %all_to_all.38.refs_0_, f32[16,1152]{1,0:T(8,128)S(1)} %get-tuple-element.41.refs_1_, f32[16,1152]{1,0:T(8,128)S(1)} %collective-permute-done.2.refs_2_, ...), custom_call_target="tpu_custom_call" | custom-call | tf_op jit(solution)/shard_map/pallas_call | solution.py:603
  41.6 0.4 collective-permute-start.3
  42.0 7.4 %all_to_all.39.recv_ref = f32[8,8,256]{2,1,0:T(8,128)S(1)} all-to-all(f32[8,8,256]{2,1,0:T(8,128)S(1)} %get-tuple-element.45), channel_id=1, replica_groups=mesh['wide'=4,'narrow'=8] {'narrow'}, dimensions={0} | all-to-all | bytes 131072 | tf_op jit(solution)/shard_map/all_to_all | solution.py:511
  49.4 3.7 %shard_map.97 = (f32[16,1024]{1,0:T(8,128)S(1)}, f32[16,1152]{1,0:T(8,128)S(1)}, f32[8,8,256]{2,1,0:T(8,128)}, f32[8,128]{1,0:T(8,128)S(1)}) custom-call(f32[8,8,256]{2,1,0:T(8,128)S(1)} %all_to_all.39.recv_ref, f32[16,1152]{1,0:T(8,128)S(1)} %get-tuple-element.46.half_ref, f32[16,1152]{1,0:T(8,128)S(1)} %collective-permute-done.3.later_ref, ...), custom_call_target="tpu_custom_call" | custom-call | tf_op jit(solution)/shard_map/pallas_call | solution.py:615
  53.1 1.6 %collective-permute-start.4 = (f32[16,1152]{1,0:T(8,128)S(1)}, f32[16,1152]{1,0:T(8,128)S(1)}, u32[]{:S(2)}, u32[]{:S(2)}) collective-permute-start(f32[16,1152]{1,0:T(8,128)S(1)} %get-tuple-element.51), channel_id=1, source_target_pairs={{0,8},{8,0},{16,24},{24,16},{1,9},{9,1},{17,25},{25,17},{2,10},{10... | collective-permute-start | bytes 221192 | tf_op jit(solution)/shard_map/ppermute | solution.py:508
  54.7 3.4 %all-to-all-start.4 = ((f32[8,8,256]{2,1,0:T(8,128)}), f32[8,8,256]{2,1,0:T(8,128)S(1)}, u32[]{:S(2)}, u32[]{:S(2)}) async-start(f32[8,8,256]{2,1,0:T(8,128)} %get-tuple-element.48), calls=%async_computation.4 | async-start | bytes 131072 | tf_op jit(solution)/shard_map/all_to_all | solution.py:511
  58.1 2.7 %collective-permute-start.5 = (f32[16,512]{1,0:T(8,128)S(1)}, f32[16,512]{1,0:T(8,128)S(1)}, u32[]{:S(2)}, u32[]{:S(2)}) collective-permute-start(f32[16,512]{1,0:T(8,128)S(1)} %get-tuple-element.56), channel_id=1, source_target_pairs={{0,16},{8,24},{16,0},{24,8},{1,17},{9,25},{17,1},{25,9},{2,18},{10... | collective-permute-start | bytes 98312 | tf_op jit(solution)/shard_map/ppermute | solution.py:508
  60.8 2.2 %all-to-all-done.4.refs_0_ = f32[8,8,256]{2,1,0:T(8,128)S(1)} async-done(((f32[8,8,256]{2,1,0:T(8,128)}), f32[8,8,256]{2,1,0:T(8,128)S(1)}, u32[]{:S(2)}, u32[]{:S(2)}) %all-to-all-start.4) | async-done | bytes 65568 | tf_op jit(solution)/shard_map/all_to_all | solution.py:511
  63.0 0.4 shard_map.98.src2
  63.5 0.1 iota.7.side_ref
  63.5 0.3 shard_map.99
  63.8 2.6 %collective-permute-start.6 = (f32[16,512]{1,0:T(8,128)S(1)}, f32[16,512]{1,0:T(8,128)S(1)}, u32[]{:S(2)}, u32[]{:S(2)}) collective-permute-start(f32[16,512]{1,0:T(8,128)S(1)} %get-tuple-element.55.kept), channel_id=1, source_target_pairs={{0,16},{8,24},{16,0},{24,8},{1,17},{9,25},{17,1},{25,9},{2,18},{10... | collective-permute-start | bytes 98312 | tf_op jit(solution)/shard_map/ppermute | solution.py:508
  66.4 10.0 %all_to_all.40 = f32[32,1,128]{2,1,0:T(1,128)S(1)} all-to-all(f32[32,1,128]{2,1,0:T(1,128)S(1)} %bitcast.15), channel_id=1, replica_groups=mesh['wide'=4,'narrow'=8] {'wide','narrow'}, dimensions={0} | all-to-all | bytes 32768 | tf_op jit(solution)/shard_map/all_to_all | solution.py:638
  76.4 0.9 %shard_map.100 = (f32[5,2048]{1,0:T(8,128)}, f32[16,1024]{1,0:T(8,128)}, f32[5,2048]{1,0:T(8,128)}, f32[16,1024]{1,0:T(8,128)}) custom-call(f32[32,128]{1,0:T(8,128)S(1)} %bitcast.14, f32[8,128]{1,0:T(8,128)S(1)} %get-tuple-element.53.scale_ref, f32[8,128]{1,0:T(8,128)S(1)} %iota.7.side_ref, f32[8,2048]{1,0:T(8,128)S(1)} %get-tuple-element.32.src0, ...), custom_call_target="tpu_custom_call" | custom-call | tf_op jit(solution)/shard_map/pallas_call | solution.py:640
  (10 shorter events, 0.0 us)
Async XLA Ops:
  6.6 11.6 %collective-permute-start = (f32[16,1152]{1,0:T(8,128)S(1)}, f32[16,1152]{1,0:T(8,128)S(1)}, u32[]{:S(2)}, u32[]{:S(2)}) collective-permute-start(f32[16,1152]{1,0:T(8,128)S(1)} %get-tuple-element.31.refs_1_), channel_id=1, source_target_pairs={{0,8},{8,0},{16,24},{24,16},{1,9},{9,1},{17,25},{25,17},{2,10},{10... | collective-permute-start | bytes 221192 | tf_op jit(solution)/shard_map/ppermute | solution.py:508
  19.7 10.0 %collective-permute-start.1 = (f32[16,1152]{1,0:T(8,128)S(1)}, f32[16,1152]{1,0:T(8,128)S(1)}, u32[]{:S(2)}, u32[]{:S(2)}) collective-permute-start(f32[16,1152]{1,0:T(8,128)S(1)} %get-tuple-element.34.half_ref), channel_id=1, source_target_pairs={{0,16},{8,24},{16,0},{24,8},{1,17},{9,25},{17,1},{25,9},{2,18},{10... | collective-permute-start | bytes 221192 | tf_op jit(solution)/shard_map/ppermute | solution.py:508
  32.6 7.9 %collective-permute-start.2 = (f32[16,1152]{1,0:T(8,128)S(1)}, f32[16,1152]{1,0:T(8,128)S(1)}, u32[]{:S(2)}, u32[]{:S(2)}) collective-permute-start(f32[16,1152]{1,0:T(8,128)S(1)} %get-tuple-element.41.refs_1_), channel_id=1, source_target_pairs={{0,8},{8,0},{16,24},{24,16},{1,9},{9,1},{17,25},{25,17},{2,10},{10... | collective-permute-start | bytes 221192 | tf_op jit(solution)/shard_map/ppermute | solution.py:508
  41.6 7.8 %collective-permute-start.3 = (f32[16,1152]{1,0:T(8,128)S(1)}, f32[16,1152]{1,0:T(8,128)S(1)}, u32[]{:S(2)}, u32[]{:S(2)}) collective-permute-start(f32[16,1152]{1,0:T(8,128)S(1)} %get-tuple-element.46.half_ref), channel_id=1, source_target_pairs={{0,16},{8,24},{16,0},{24,8},{1,17},{9,25},{17,1},{25,9},{2,18},{10... | collective-permute-start | bytes 221192 | tf_op jit(solution)/shard_map/ppermute | solution.py:508
  53.1 5.0 %collective-permute-start.4 = (f32[16,1152]{1,0:T(8,128)S(1)}, f32[16,1152]{1,0:T(8,128)S(1)}, u32[]{:S(2)}, u32[]{:S(2)}) collective-permute-start(f32[16,1152]{1,0:T(8,128)S(1)} %get-tuple-element.51), channel_id=1, source_target_pairs={{0,8},{8,0},{16,24},{24,16},{1,9},{9,1},{17,25},{25,17},{2,10},{10... | collective-permute-start | bytes 221192 | tf_op jit(solution)/shard_map/ppermute | solution.py:508
  54.7 8.3 %all-to-all-start.4 = ((f32[8,8,256]{2,1,0:T(8,128)}), f32[8,8,256]{2,1,0:T(8,128)S(1)}, u32[]{:S(2)}, u32[]{:S(2)}) async-start(f32[8,8,256]{2,1,0:T(8,128)} %get-tuple-element.48), calls=%async_computation.4 | async-start | bytes 131072 | tf_op jit(solution)/shard_map/all_to_all | solution.py:511
  58.1 5.3 %collective-permute-start.5 = (f32[16,512]{1,0:T(8,128)S(1)}, f32[16,512]{1,0:T(8,128)S(1)}, u32[]{:S(2)}, u32[]{:S(2)}) collective-permute-start(f32[16,512]{1,0:T(8,128)S(1)} %get-tuple-element.56), channel_id=1, source_target_pairs={{0,16},{8,24},{16,0},{24,8},{1,17},{9,25},{17,1},{25,9},{2,18},{10... | collective-permute-start | bytes 98312 | tf_op jit(solution)/shard_map/ppermute | solution.py:508
  63.8 12.6 %collective-permute-start.6 = (f32[16,512]{1,0:T(8,128)S(1)}, f32[16,512]{1,0:T(8,128)S(1)}, u32[]{:S(2)}, u32[]{:S(2)}) collective-permute-start(f32[16,512]{1,0:T(8,128)S(1)} %get-tuple-element.55.kept), channel_id=1, source_target_pairs={{0,16},{8,24},{16,0},{24,8},{1,17},{9,25},{17,1},{25,9},{2,18},{10... | collective-permute-start | bytes 98312 | tf_op jit(solution)/shard_map/ppermute | solution.py:508
